TPU v7x, 256 devices: a whole 4x4x8 slice. The times are simulated.
256 devices in a mesh: dp: 32 (over y, z), segment: 2 (over x_lo), chan: 4 (over x_hi, core).
Axes of the slice: x: 4 (x_hi: 2, x_lo: 2; x = x_hi * 2 + x_lo), y: 4, z: 8, core: 2. Of those that a mesh axis runs over, the one named last changes fastest.
Arguments:
- base: bfloat16 [64, 512, 256], P('dp', 'chan'), may hold values from -6 to 6
- style: float32 [2, 64, 512], P('segment', 'dp'), may hold values from -3 to 3
- noise: float32 [2, 64, 256], P('segment', 'dp'), may hold values from -6 to 6
- conv_weight: bfloat16 [2, 4608, 512], P('segment', None, 'chan'), may hold values from -0.09375 to 0.09375
- conv_bias: float32 [2, 512], P('segment', 'chan'), may hold values from -3 to 3
- noise_gain: float32 [2, 512], P('segment', 'chan'), may hold values from 0.1 to 1
- rgb_weight: bfloat16 [2, 3, 512], P('segment', None, 'chan'), may hold values from -0.25 to 0.25
- disc_weight: float32 [3, 256], replicated, may hold values from -3.5 to 3.5
- disc_bias: float32 [256], replicated, may hold values from -3 to 3
- disc_out: float32 [256], replicated, may hold values from -3 to 3
Outputs:
- conv_grad: float32 [2, 4608, 512], P('segment', 'dp', 'chan')
- logits: float32 [64], P('dp')
- section_input_grads: bfloat16 [2, 64, 512, 256], P('segment', 'dp', 'chan')
All inputs are finite; a program needn't handle non-finite values.
Results may differ from a plain program's by a relative error of at most 0.015.
Values may be sent and summed in bfloat16 or wider, within the bound.
No kernel may reach another device: no remote copies, remote signals or barrier semaphores. Data moves between devices by JAX's collectives and lax.ppermute only.
A program may use at most 64 MiB of HBM per device.

v0:
```python
import jax
import jax.numpy as jnp
from jax import lax
from jax.sharding import PartitionSpec as P

RES = 16
epsilon = 1e-06
root_two = 1.4142135623730951
highest = lax.Precision.HIGHEST
kernel_offsets = [(ky - 1, kx - 1) for ky in range(3) for kx in range(3)]


def shifted(value, axis, steps):
    count = lax.axis_size(axis)
    first, last = (max(0, -steps), min(count, count - steps))
    return lax.ppermute(value, axis, [(source, source + steps) for source in range(first, last)])


def leaky_relu(values):
    return 0.2 * values + 0.8 * jax.nn.softplus(values)


def leaky_slope(values):
    return 0.2 + 0.8 * jax.nn.sigmoid(values)


def shift_grid(values, offset_y, offset_x):
    leading = values.shape[:-1]
    planes = values.reshape(leading + (RES, RES))
    padded = jnp.pad(planes, [(0, 0)] * len(leading) + [(1, 1), (1, 1)])
    moved = padded[..., 1 + offset_y : 1 + offset_y + RES, 1 + offset_x : 1 + offset_x + RES]
    return moved.reshape(leading + (RES * RES,))


def store_slot(buffer, item, slot_clip, is_valid, axis_pos, width):
    offset = slot_clip * width
    previous = lax.dynamic_slice_in_dim(buffer, offset, width, axis_pos)
    return lax.dynamic_update_slice_in_dim(
        buffer, jnp.where(is_valid, item, previous), offset, axis_pos
    )


def shards(
    base,
    style,
    noise,
    conv_weight,
    conv_bias,
    noise_gain,
    rgb_weight,
    disc_weight,
    disc_bias,
    disc_out,
):
    weight = conv_weight[0]
    full_width = weight.shape[0] // 9
    own_width = weight.shape[1]
    micro_count = base.shape[0]
    pixels = base.shape[2]
    segment_index = lax.axis_index("segment")
    chan_index = lax.axis_index("chan")
    styles = style[0]
    own_styles = lax.dynamic_slice_in_dim(styles, chan_index * own_width, own_width, 1)
    w_float = weight.astype(jnp.float32)
    squares = jnp.sum((w_float * w_float).reshape(9, full_width, own_width), axis=0)
    style_sq = styles * styles
    demods = lax.rsqrt(
        jnp.dot(style_sq, squares, precision=highest, preferred_element_type=jnp.float32) + epsilon
    )
    bias_row = conv_bias[0]
    gain_row = noise_gain[0]
    noises = noise[0]
    rgb_proj = rgb_weight[0]
    columns_all = jnp.zeros((9 * full_width, micro_count * pixels), jnp.bfloat16)
    pre_all = jnp.zeros((micro_count, own_width, pixels), jnp.float32)
    conv_all = jnp.zeros((micro_count, own_width, pixels), jnp.float32)
    image_part = jnp.zeros((micro_count, 3, pixels), jnp.float32)
    outgoing = jnp.zeros((own_width, pixels), jnp.bfloat16)
    for tick_index in range(micro_count + 1):
        slot_index = tick_index - segment_index
        is_valid = (slot_index >= 0) & (slot_index < micro_count)
        slot_clip = jnp.clip(slot_index, 0, micro_count - 1)
        if tick_index > 0:
            incoming = shifted(outgoing, "segment", 1)
        else:
            incoming = outgoing
        first_input = lax.dynamic_index_in_dim(base, slot_clip, 0, keepdims=False)
        inputs = jnp.where(segment_index == 0, first_input, incoming)
        style_row = lax.dynamic_index_in_dim(own_styles, slot_clip, 0, keepdims=False)
        demod_row = lax.dynamic_index_in_dim(demods, slot_clip, 0, keepdims=False)
        noise_row = lax.dynamic_index_in_dim(noises, slot_clip, 0, keepdims=False)
        modulated = (inputs.astype(jnp.float32) * style_row[:, None]).astype(jnp.bfloat16)
        gathered = lax.all_gather(modulated, "chan", axis=0, tiled=True)
        columns = jnp.concatenate(
            [shift_grid(gathered, oy, ox) for oy, ox in kernel_offsets], axis=0
        )
        conv_out = lax.dot_general(
            weight, columns, (((0,), (0,)), ((), ())), preferred_element_type=jnp.float32
        )
        pre_act = (
            demod_row[:, None] * conv_out
            + gain_row[:, None] * noise_row[None, :]
            + bias_row[:, None]
        )
        out_act = (root_two * leaky_relu(pre_act)).astype(jnp.bfloat16)
        rgb_part = jnp.dot(rgb_proj, out_act, preferred_element_type=jnp.float32)
        columns_all = store_slot(columns_all, columns, slot_clip, is_valid, 1, pixels)
        pre_all = store_slot(pre_all, pre_act[None], slot_clip, is_valid, 0, 1)
        conv_all = store_slot(conv_all, conv_out[None], slot_clip, is_valid, 0, 1)
        image_part = store_slot(image_part, rgb_part[None], slot_clip, is_valid, 0, 1)
        outgoing = out_act
    images = lax.psum(image_part, ("segment", "chan"))
    pre_disc = (
        jnp.einsum("cj,mcp->mjp", disc_weight, images, precision=highest) + disc_bias[None, :, None]
    )
    hidden = leaky_relu(pre_disc)
    logits = jnp.dot(
        jnp.mean(hidden, axis=2), disc_out, precision=highest, preferred_element_type=jnp.float32
    )
    grad_logit = jax.nn.sigmoid(logits) - 1.0
    d_pre = grad_logit[:, None, None] * disc_out[None, :, None] / pixels * leaky_slope(pre_disc)
    d_image = jnp.einsum("cj,mjp->mcp", disc_weight, d_pre, precision=highest)
    head_grad = jnp.einsum("co,mcp->mop", rgb_proj.astype(jnp.float32), d_image, precision=highest)
    grads_all = jnp.zeros((own_width, micro_count * pixels), jnp.bfloat16)
    coef_all = jnp.zeros((micro_count, own_width), jnp.float32)
    returned_all = jnp.zeros((micro_count, own_width, pixels), jnp.bfloat16)
    returned = jnp.zeros((own_width, pixels), jnp.bfloat16)
    for tick_index in range(micro_count + 1):
        slot_index = tick_index - 1 + segment_index
        is_valid = (slot_index >= 0) & (slot_index < micro_count)
        slot_clip = jnp.clip(slot_index, 0, micro_count - 1)
        if tick_index > 0:
            incoming = shifted(returned, "segment", -1)
        else:
            incoming = returned
        style_row = lax.dynamic_index_in_dim(own_styles, slot_clip, 0, keepdims=False)
        demod_row = lax.dynamic_index_in_dim(demods, slot_clip, 0, keepdims=False)
        pre_act = lax.dynamic_index_in_dim(pre_all, slot_clip, 0, keepdims=False)
        conv_out = lax.dynamic_index_in_dim(conv_all, slot_clip, 0, keepdims=False)
        grad_out = lax.dynamic_index_in_dim(
            head_grad, slot_clip, 0, keepdims=False
        ) + incoming.astype(jnp.float32)
        d_act = grad_out * root_two * leaky_slope(pre_act)
        d_conv = (d_act * demod_row[:, None]).astype(jnp.bfloat16)
        d_demod = jnp.sum(d_act * conv_out, axis=1)
        coef_row = -d_demod * demod_row * demod_row * demod_row
        grads_all = store_slot(grads_all, d_conv, slot_clip, is_valid, 1, pixels)
        coef_all = store_slot(coef_all, coef_row[None], slot_clip, is_valid, 0, 1)
        total = jnp.zeros((own_width * lax.axis_size("chan"), pixels), jnp.float32)
        for kernel_pos, (input_oy, input_ox) in enumerate(kernel_offsets):
            weight_rows = lax.dynamic_slice_in_dim(
                weight, kernel_pos * full_width, own_width * lax.axis_size("chan"), 0
            )
            piece_out = lax.dot_general(
                weight_rows, d_conv, (((1,), (0,)), ((), ())), preferred_element_type=jnp.float32
            )
            total = total + shift_grid(piece_out, -input_oy, -input_ox)
        d_input = lax.psum_scatter(total, "chan", scatter_dimension=0, tiled=True)
        returned = (d_input * style_row[:, None]).astype(jnp.bfloat16)
        returned_all = store_slot(returned_all, returned[None], slot_clip, is_valid, 0, 1)
    demod_total = jnp.dot(
        style_sq.T, coef_all, precision=highest, preferred_element_type=jnp.float32
    )
    demod_term = (w_float.reshape(9, full_width, own_width) * demod_total[None]).reshape(
        9 * full_width, own_width
    )
    local_grad = lax.dot_general(
        columns_all, grads_all, (((1,), (1,)), ((), ())), preferred_element_type=jnp.float32
    )
    grad_rows = lax.psum_scatter(
        (local_grad + demod_term).astype(jnp.bfloat16), "dp", scatter_dimension=0, tiled=True
    ).astype(jnp.float32)
    return (grad_rows[None], logits, returned_all[None])


def solution(mesh):
    placed = (
        P("dp", "chan", None),
        P("segment", "dp", None),
        P("segment", "dp", None),
        P("segment", None, "chan"),
        P("segment", "chan"),
        P("segment", "chan"),
        P("segment", None, "chan"),
        P(),
        P(),
        P(),
    )
    return jax.shard_map(
        shards,
        mesh=mesh,
        in_specs=placed,
        out_specs=(P("segment", "dp", "chan"), P("dp"), P("segment", "dp", "chan", None)),
        check_vma=False,
    )
```

profile of v0, /device:TPU:4, one launch (start us, length us, event | category | flops | bytes accessed | tf_op | source)
XLA Modules:
  0.0 444.8 jit_solution(5828866508853112083)
XLA Ops:
  7.3 1.6 constant_dynamic-slice_fusion.15
  9.0 1.6 fusion.192
  10.6 7.3 %all_gather.9 = bf16[512,256]{0,1:T(8,128)(2,1)S(1)} all-gather(bf16[128,256]{0,1:T(8,128)(2,1)S(1)} %fusion.71), channel_id=1, replica_groups=mesh['dp'=32,'segment'=2,'chan'=4] {'chan'}, dimensions={0}, use_global_device_ids=true | all-gather | bytes 327680 | tf_op jit(solution)/shard_map/all_gather | solution.py:93
  21.1 2.5 reduce_sum.45
  33.6 3.7 collective-permute-start
  39.8 1.6 copy.14
  43.9 7.3 %all_gather.10 = bf16[512,256]{0,1:T(8,128)(2,1)S(1)} all-gather(bf16[128,256]{0,1:T(8,128)(2,1)S(1)} %multiply_convert_fusion.7), channel_id=1, replica_groups=mesh['dp'=32,'segment'=2,'chan'=4] {'chan'}, dimensions={0}, use_global_device_ids=true | all-gather | bytes 327680 | tf_op jit(solution)/shard_map/all_gather | solution.py:93
  52.1 2.8 fusion.66
  56.6 2.0 collective-permute-done.1
  58.6 7.3 %all_gather.11 = bf16[512,256]{0,1:T(8,128)(2,1)S(1)} all-gather(bf16[128,256]{0,1:T(8,128)(2,1)S(1)} %multiply_convert_fusion.6), channel_id=1, replica_groups=mesh['dp'=32,'segment'=2,'chan'=4] {'chan'}, dimensions={0}, use_global_device_ids=true | all-gather | bytes 327680 | tf_op jit(solution)/shard_map/all_gather | solution.py:93
  67.9 2.5 fusion.65
  70.7 14.6 %psum.7 = f32[2,3,256]{2,1,0:T(4,128)} all-reduce(f32[2,3,256]{2,1,0:T(4,128)S(1)} %fusion.26), channel_id=1, replica_groups=mesh['dp'=32,'segment'=2,'chan'=4] {'segment','chan'}, use_global_device_ids=true, to_apply=%region_1.2 | all-reduce | flops 1536 | bytes 12288 | tf_op jit(solution)/shard_map/psum | solution.py:112
  85.2 1.6 fusion.41
  94.7 35.7 %reduce-scatter.5.cloned.1.call-done = f32[128,256]{0,1:T(8,128)} async-done(((f32[512,256]{0,1:T(8,128)}), f32[128,256]{0,1:T(8,128)}) %reduce-scatter.5.cloned.1.call-update) | async-done | bytes 131088 | tf_op jit(solution)/shard_map/reduce_scatter | solution.py:158
  134.1 2.4 broadcast_in_dim.35
  136.6 1.8 select_dynamic-update-slice_fusion.2
  139.1 1.8 select_dynamic-update-slice_fusion.4
  145.1 3.7 select_dynamic-update-slice_fusion.1
  148.8 30.0 %reduce-scatter.7.cloned.1.call-done = f32[128,256]{0,1:T(8,128)} async-done(((f32[512,256]{0,1:T(8,128)}), f32[128,256]{0,1:T(8,128)}) %reduce-scatter.7.cloned.1.call-update) | async-done | bytes 131088 | tf_op jit(solution)/shard_map/reduce_scatter | solution.py:158
  178.8 1.6 fusion.168
  181.8 3.6 select_dynamic-update-slice_fusion
  193.3 4.9 %fusion = bf16[4608,128]{1,0:T(8,128)(2,1)} fusion(f32[4608,128]{1,0:T(8,128)S(1)} %bitcast_multiply_fusion, bf16[4608,512]{0,1:T(8,128)(2,1)} %select_dynamic-update-slice_fusion, bf16[128,512]{0,1:T(8,128)(2,1)S(1)} %get-tuple-element.13), kind=kOutput, calls=%fused_computation.1 | convolution fusion | flops 605159424 | bytes 8388608 | tf_op jit(solution)/shard_map/dot_general | solution.py:167
  199.2 26.3 %reduce-scatter.11.cloned.1.call-done = f32[128,256]{0,1:T(8,128)} async-done(((f32[512,256]{0,1:T(8,128)}), f32[128,256]{0,1:T(8,128)}) %reduce-scatter.11.cloned.1.call-update) | async-done | bytes 131088 | tf_op jit(solution)/shard_map/reduce_scatter | solution.py:158
  227.1 209.8 %reduce-scatter.9.cloned.1.call-done = bf16[144,128]{1,0:T(8,128)(2,1)} async-done(((bf16[4608,128]{1,0:T(8,128)(2,1)}), bf16[144,128]{1,0:T(8,128)(2,1)}) %reduce-scatter.9.cloned.1.call-update) | async-done | bytes 36880 | tf_op jit(solution)/shard_map/reduce_scatter | solution.py:170
  (203 shorter events, 52.1 us)
Async XLA Ops:
  7.2 78.1 %copy-start = (f32[3,256]{1,0:T(4,128)S(1)}, f32[3,256]{1,0:T(4,128)}, u32[]{:S(2)}) copy-start(f32[3,256]{1,0:T(4,128)} %param.17) | copy-start | bytes 9220
  7.2 123.2 %reduce-scatter.5.cloned.1.call-start = ((), (), s32[]{:S(2)}) async-start(), calls=%async_computation.4 | async-start | bytes 655360 | tf_op jit(solution)/shard_map/reduce_scatter | solution.py:158
  19.5 5.9 %copy-start.29 = (f32[1,2,256]{2,1,0:T(2,128)S(1)}, f32[1,2,256]{2,1,0:T(2,128)}, u32[]{:S(2)}) copy-start(f32[1,2,256]{2,1,0:T(2,128)} %param.12) | copy-start | bytes 6148
  30.0 8.1 %copy-start.25 = (f32[1,1,256]{2,1,0:T(1,128)S(1)}, f32[1,1,256]{2,1,0:T(1,128)}, u32[]{:S(2)}) copy-start(f32[1,1,256]{2,1,0:T(1,128)} %get-tuple-element.59) | copy-start | bytes 3076
  30.0 8.1 %copy-start.28 = (f32[128]{0:T(128)S(1)}, f32[128]{0:T(128)}, u32[]{:S(2)}) copy-start(f32[128]{0:T(128)} %get-tuple-element.66) | copy-start | bytes 1540
  30.0 8.9 %copy-start.22 = (bf16[1,3,128]{2,1,0:T(4,128)(2,1)S(1)}, bf16[1,3,128]{2,1,0:T(4,128)(2,1)}, u32[]{:S(2)}) copy-start(bf16[1,3,128]{2,1,0:T(4,128)(2,1)} %param.16) | copy-start | bytes 2308
  33.6 9.3 %collective-permute-start = (bf16[128,256]{0,1:T(8,128)(2,1)}, bf16[128,256]{0,1:T(8,128)(2,1)}, u32[]{:S(2)}, u32[]{:S(2)}) collective-permute-start(bf16[128,256]{0,1:T(8,128)(2,1)} %fusion.56), channel_id=1, source_target_pairs={{0,4},{1,5},{2,6},{3,7},{8,12},{9,13},{10,14},{11,15},{16,20},{17,... | collective-permute-start | bytes 196616 | tf_op jit(solution)/shard_map/ppermute | solution.py:16
  51.7 14.2 %copy-start.2 = (bf16[4608,256]{0,1:T(8,128)(2,1)}, bf16[4608,256]{0,1:T(8,128)(2,1)S(1)}, u32[]{:S(2)}) copy-start(bf16[4608,256]{0,1:T(8,128)(2,1)S(1)} %constant_dynamic-update-slice_fusion.9) | copy-start | bytes 7077892
  51.8 6.8 %copy-start.12 = (bf16[1,128,256]{1,2,0:T(8,128)(2,1)S(1)}, bf16[1,128,256]{1,2,0:T(8,128)(2,1)}, u32[]{:S(2)}) copy-start(bf16[1,128,256]{1,2,0:T(8,128)(2,1)} %copy.15) | copy-start | bytes 196612
  51.8 6.8 %copy-start.36 = (f32[128]{0:T(128)S(1)}, f32[128]{0:T(128)}, u32[]{:S(2)}) copy-start(f32[128]{0:T(128)} %get-tuple-element.54) | copy-start | bytes 1540
  55.1 3.4 collective-permute-start.1
  70.4 19.3 %copy-start.24 = (bf16[1,3,128]{2,1,0:T(4,128)(2,1)S(1)}, bf16[1,3,128]{2,1,0:T(4,128)(2,1)}, u32[]{:S(2)}) copy-start(bf16[1,3,128]{2,1,0:T(4,128)(2,1)} %param.16) | copy-start | bytes 2308
  85.2 4.9 %copy-start.27 = (f32[128]{0:T(128)S(1)}, f32[128]{0:T(128)}, u32[]{:S(2)}) copy-start(f32[128]{0:T(128)} %get-tuple-element.63) | copy-start | bytes 1540
  93.6 37.5 %copy-start.35 = (f32[128]{0:T(128)S(1)}, f32[128]{0:T(128)}, u32[]{:S(2)}) copy-start(f32[128]{0:T(128)} %get-tuple-element.53) | copy-start | bytes 1540
  94.6 84.2 %reduce-scatter.7.cloned.1.call-start = ((), (), s32[]{:S(2)}) async-start(), calls=%async_computation.5 | async-start | bytes 655360 | tf_op jit(solution)/shard_map/reduce_scatter | solution.py:158
  132.7 6.5 %collective-permute-start.2 = (bf16[128,256]{0,1:T(8,128)(2,1)}, bf16[128,256]{0,1:T(8,128)(2,1)}, u32[]{:S(2)}, u32[]{:S(2)}) collective-permute-start(bf16[128,256]{0,1:T(8,128)(2,1)} %get-tuple-element.12), channel_id=1, source_target_pairs={{4,0},{5,1},{6,2},{7,3},{12,8},{13,9},{14,10},{15,11},{20,16},{21,... | collective-permute-start | bytes 196616 | tf_op jit(solution)/shard_map/ppermute | solution.py:16
  144.3 34.5 %copy-start.32 = (f32[128]{0:T(128)S(1)}, f32[128]{0:T(128)}, u32[]{:S(2)}) copy-start(f32[128]{0:T(128)} %get-tuple-element.57) | copy-start | bytes 1540
  144.3 81.1 %reduce-scatter.11.cloned.1.call-start = ((), (), s32[]{:S(2)}) async-start(), calls=%async_computation.7 | async-start | bytes 655360 | tf_op jit(solution)/shard_map/reduce_scatter | solution.py:158
  180.4 6.3 %copy-start.6 = (f32[2,256,128]{2,1,0:T(8,128)S(1)}, f32[2,256,128]{2,1,0:T(8,128)}, u32[]{:S(2)}) copy-start(f32[2,256,128]{2,1,0:T(8,128)} %copy-done.5) | copy-start | bytes 786436
  180.4 6.3 %copy-start.8 = (bf16[128,512]{0,1:T(8,128)(2,1)S(1)}, bf16[128,512]{0,1:T(8,128)(2,1)}, u32[]{:S(2)}) copy-start(bf16[128,512]{0,1:T(8,128)(2,1)} %get-tuple-element.16) | copy-start | bytes 393220
  180.4 6.3 %copy-start.33 = (f32[128]{0:T(128)S(1)}, f32[128]{0:T(128)}, u32[]{:S(2)}) copy-start(f32[128]{0:T(128)} %get-tuple-element.61) | copy-start | bytes 1540
  180.4 6.3 %collective-permute-start.3 = (bf16[128,256]{0,1:T(8,128)(2,1)S(1)}, bf16[128,256]{0,1:T(8,128)(2,1)S(1)}, u32[]{:S(2)}, u32[]{:S(2)}) collective-permute-start(bf16[128,256]{0,1:T(8,128)(2,1)S(1)} %get-tuple-element.10), channel_id=1, source_target_pairs={{4,0},{5,1},{6,2},{7,3},{12,8},{13,9},{14,10},{15,11},{20,16},{21,... | collective-permute-start | bytes 196616 | tf_op jit(solution)/shard_map/ppermute | solution.py:16
  191.2 245.7 %reduce-scatter.9.cloned.1.call-start = ((), (), s32[]{:S(2)}) async-start(), calls=%async_computation.6 | async-start | bytes 1216512 | tf_op jit(solution)/shard_map/reduce_scatter | solution.py:170
  193.3 32.1 %copy-start.31 = (f32[128]{0:T(128)S(1)}, f32[128]{0:T(128)}, u32[]{:S(2)}) copy-start(f32[128]{0:T(128)} %get-tuple-element.52) | copy-start | bytes 1540
  (21 other events, 45.3 us)
Sparse Core Ops, SparseCore 0:
  94.8 35.6 reduce-scatter.4
  144.4 34.3 reduce-scatter.6
  191.3 34.1 reduce-scatter.10
  229.1 207.7 reduce-scatter.8
where the time goes:
time: 446 us; the launch traced here: 445 us
  waiting for transfers between devices  306 us (69%)
  blocking collectives  36.5 us (8%)
  other arithmetic  28.7 us (6%)
  matrix products  27.4 us (6%)
  local copies, waits for them, and re-layouts  23.6 us (5%)
  between operations  14.8 us (3%)
  starting transfers between devices  8.04 us (2%)
    reduce_scatter x1, waiting for transfers between devices, shards(): lax.psum_scatter((local_grad + demod_term).astype(jnp.bfloat16), 'dp', sc...  210 us
    reduce_scatter x3, waiting for transfers between devices, shards(): d_input = lax.psum_scatter(total, 'chan', scatter_dimension=0, tiled=True)  92 us
    all_gather x3, blocking collectives, shards(): gathered = lax.all_gather(modulated, 'chan', axis=0, tiled=True)  21.9 us
    dynamic_update_slice x10, other arithmetic, store_slot(): lax.dynamic_update_slice_in_dim(buffer, jnp.where(is_valid, item, previou...  17.9 us
    psum x1, blocking collectives, shards(): images = lax.psum(image_part, ('segment', 'chan'))  14.6 us
  transfers between devices with their start and end apart: 8, of which 7 were waited for; matrix products, arithmetic and copies ran while one was open for 6% of the time, Pallas kernels for 0%

commit v1 on v0

--- a/solution.py
+++ b/solution.py
@@ -90,7 +90,8 @@
         demod_row = lax.dynamic_index_in_dim(demods, slot_clip, 0, keepdims=False)
         noise_row = lax.dynamic_index_in_dim(noises, slot_clip, 0, keepdims=False)
         modulated = (inputs.astype(jnp.float32) * style_row[:, None]).astype(jnp.bfloat16)
-        gathered = lax.all_gather(modulated, "chan", axis=0, tiled=True)
+        repeated = jnp.stack([modulated] * lax.axis_size("chan"))
+        gathered = jnp.concatenate(lax.all_to_all(repeated, "chan", 0, 0), axis=0)
         columns = jnp.concatenate(
             [shift_grid(gathered, oy, ox) for oy, ox in kernel_offsets], axis=0
         )

time: 446 us -> 460 us (1.031)
  blocking collectives: 36.5 us -> 16.2 us
  starting transfers between devices: 8.04 us -> 27.3 us
  local copies, waits for them, and re-layouts: 23.6 us -> 34.4 us
  waiting for transfers between devices: 306 us -> 314 us
    all_gather x3 -> x0, blocking collectives: 21.9 us -> none  [shards(): gathered = lax.all_gather(modulated, 'chan', axis=0, tiled=True)]
    all_to_all x0 -> x3, starting transfers between devices: none -> 18.7 us  [shards(): gathered = jnp.concatenate(lax.all_to_all(repeated, 'chan', 0, 0), axis=0)]
    all_to_all x0 -> x3, waiting for transfers between devices: none -> 6.88 us  [shards(): gathered = jnp.concatenate(lax.all_to_all(repeated, 'chan', 0, 0), axis=0)]
    another operation x2 -> x9, local copies, waits for them, and re-layouts: 1.45 us -> 7.39 us  [the longest x3 3.64 us: shift_grid(): planes = values.reshape(leading + (RES, RES))]
    unnamed x101 -> x120, local copies, waits for them, and re-layouts: 8.09 us -> 9.29 us
  transfers between devices with their start and end apart: 8 -> 11, of which waited for: 7 -> 10; matrix products, arithmetic and copies ran while one was open for 6% -> 6% of each run, Pallas kernels for 0% -> 0%
where the time goes in v1:
time: 460 us; the launch traced here: 459 us
  waiting for transfers between devices  314 us (68%)
  local copies, waits for them, and re-layouts  34.4 us (7%)
  starting transfers between devices  27.3 us (6%)
  matrix products  27.1 us (6%)
  other arithmetic  25.5 us (6%)
  blocking collectives  16.2 us (4%)
  between operations  15 us (3%)
    reduce_scatter x1, waiting for transfers between devices, shards(): lax.psum_scatter((local_grad + demod_term).astype(jnp.bfloat16), 'dp', sc...  210 us
    reduce_scatter x3, waiting for transfers between devices, shards(): d_input = lax.psum_scatter(total, 'chan', scatter_dimension=0, tiled=True)  90.9 us
    all_to_all x3, starting transfers between devices, shards(): gathered = jnp.concatenate(lax.all_to_all(repeated, 'chan', 0, 0), axis=0)  18.7 us
    dynamic_update_slice x10, other arithmetic, store_slot(): lax.dynamic_update_slice_in_dim(buffer, jnp.where(is_valid, item, previou...  16.9 us
    psum x1, blocking collectives, shards(): images = lax.psum(image_part, ('segment', 'chan'))  16.2 us
    unnamed x120, local copies, waits for them, and re-layouts  9.29 us
  transfers between devices with their start and end apart: 11, of which 10 were waited for; matrix products, arithmetic and copies ran while one was open for 6% of the time, Pallas kernels for 0%

profile of v1, /device:TPU:4, one launch (start us, length us, event | category | flops | bytes accessed | tf_op | source)
XLA Modules:
  0.0 459.0 jit_solution(5838010167549405489)
XLA Ops:
  10.6 5.6 %all-to-all-start = ((bf16[4,128,256]{1,2,0:T(8,128)(2,1)}), bf16[4,128,256]{1,2,0:T(8,128)(2,1)S(1)}, u32[]{:S(2)}, u32[]{:S(2)}) async-start(bf16[4,128,256]{1,2,0:T(8,128)(2,1)} %stack.9), calls=%async_computation | async-start | bytes 524288 | tf_op jit(solution)/shard_map/all_to_all | solution.py:94
  26.2 2.9 collective-permute-start
  34.6 6.5 %all-to-all-start.1 = ((bf16[4,128,256]{1,2,0:T(8,128)(2,1)}), bf16[4,128,256]{1,2,0:T(8,128)(2,1)}, u32[]{:S(2)}, u32[]{:S(2)}) async-start(bf16[4,128,256]{1,2,0:T(8,128)(2,1)} %stack.10), calls=%async_computation.1 | async-start | bytes 524288 | tf_op jit(solution)/shard_map/all_to_all | solution.py:94
  43.5 2.1 all-to-all-done.1
  45.6 1.9 copy.26
  47.4 1.7 reshape_reshape.7
  49.2 2.8 pad_slice_fusion.32
  54.6 2.5 fusion.66
  57.3 2.7 collective-permute-start.1
  62.6 6.5 %all-to-all-start.2 = ((bf16[4,128,256]{1,2,0:T(8,128)(2,1)}), bf16[4,128,256]{1,2,0:T(8,128)(2,1)}, u32[]{:S(2)}, u32[]{:S(2)}) async-start(bf16[4,128,256]{1,2,0:T(8,128)(2,1)} %stack.11), calls=%async_computation.2 | async-start | bytes 524288 | tf_op jit(solution)/shard_map/all_to_all | solution.py:94
  70.2 3.5 all-to-all-done.2
  73.7 1.8 copy.29
  75.5 1.8 reshape_reshape.8
  77.3 3.0 pad_slice_fusion.24
  83.1 2.5 fusion.65
  85.9 16.2 %psum.7 = f32[2,3,256]{2,1,0:T(4,128)} all-reduce(f32[2,3,256]{2,1,0:T(4,128)S(1)} %fusion.26), channel_id=1, replica_groups=mesh['dp'=32,'segment'=2,'chan'=4] {'segment','chan'}, use_global_device_ids=true, to_apply=%region_1.2 | all-reduce | flops 1536 | bytes 12288 | tf_op jit(solution)/shard_map/psum | solution.py:113
  111.5 35.5 %reduce-scatter.5.cloned.1.call-done = f32[128,256]{0,1:T(8,128)} async-done(((f32[512,256]{0,1:T(8,128)}), f32[128,256]{0,1:T(8,128)}) %reduce-scatter.5.cloned.1.call-update) | async-done | bytes 131088 | tf_op jit(solution)/shard_map/reduce_scatter | solution.py:159
  151.0 3.8 collective-permute-done.2
  160.7 3.8 select_dynamic-update-slice_fusion.1
  164.5 28.2 %reduce-scatter.7.cloned.1.call-done = f32[128,256]{0,1:T(8,128)} async-done(((f32[512,256]{0,1:T(8,128)}), f32[128,256]{0,1:T(8,128)}) %reduce-scatter.7.cloned.1.call-update) | async-done | bytes 131088 | tf_op jit(solution)/shard_map/reduce_scatter | solution.py:159
  195.6 3.7 select_dynamic-update-slice_fusion
  207.2 4.9 %fusion = bf16[4608,128]{1,0:T(8,128)(2,1)} fusion(f32[4608,128]{1,0:T(8,128)S(1)} %bitcast_multiply_fusion, bf16[4608,512]{0,1:T(8,128)(2,1)} %select_dynamic-update-slice_fusion, bf16[128,512]{0,1:T(8,128)(2,1)S(1)} %get-tuple-element.19), kind=kOutput, calls=%fused_computation.1 | convolution fusion | flops 605159424 | bytes 8388608 | tf_op jit(solution)/shard_map/dot_general | solution.py:168
  212.1 27.2 %reduce-scatter.11.cloned.1.call-done = f32[128,256]{0,1:T(8,128)} async-done(((f32[512,256]{0,1:T(8,128)}), f32[128,256]{0,1:T(8,128)}) %reduce-scatter.11.cloned.1.call-update) | async-done | bytes 131088 | tf_op jit(solution)/shard_map/reduce_scatter | solution.py:159
  241.1 210.0 %reduce-scatter.9.cloned.1.call-done = bf16[144,128]{1,0:T(8,128)(2,1)} async-done(((bf16[4608,128]{1,0:T(8,128)(2,1)}), bf16[144,128]{1,0:T(8,128)(2,1)}) %reduce-scatter.9.cloned.1.call-update) | async-done | bytes 36880 | tf_op jit(solution)/shard_map/reduce_scatter | solution.py:171
  (235 shorter events, 63.0 us)
Async XLA Ops:
  7.2 94.9 %copy-start = (f32[3,256]{1,0:T(4,128)S(1)}, f32[3,256]{1,0:T(4,128)}, u32[]{:S(2)}) copy-start(f32[3,256]{1,0:T(4,128)} %param.17) | copy-start | bytes 9220
  10.6 10.0 %all-to-all-start = ((bf16[4,128,256]{1,2,0:T(8,128)(2,1)}), bf16[4,128,256]{1,2,0:T(8,128)(2,1)S(1)}, u32[]{:S(2)}, u32[]{:S(2)}) async-start(bf16[4,128,256]{1,2,0:T(8,128)(2,1)} %stack.9), calls=%async_computation | async-start | bytes 524288 | tf_op jit(solution)/shard_map/all_to_all | solution.py:94
  22.5 6.6 %copy-start.20 = (bf16[2,128,256]{2,1,0:T(8,128)(2,1)S(1)}, bf16[2,128,256]{2,1,0:T(8,128)(2,1)}, u32[]{:S(2)}) copy-start(bf16[2,128,256]{2,1,0:T(8,128)(2,1)} %param.10) | copy-start | bytes 393220
  26.2 6.7 %collective-permute-start = (bf16[128,256]{0,1:T(8,128)(2,1)}, bf16[128,256]{0,1:T(8,128)(2,1)}, u32[]{:S(2)}, u32[]{:S(2)}) collective-permute-start(bf16[128,256]{0,1:T(8,128)(2,1)} %fusion.56), channel_id=1, source_target_pairs={{0,4},{1,5},{2,6},{3,7},{8,12},{9,13},{10,14},{11,15},{16,20},{17,... | collective-permute-start | bytes 196616 | tf_op jit(solution)/shard_map/ppermute | solution.py:16
  34.6 11.0 %all-to-all-start.1 = ((bf16[4,128,256]{1,2,0:T(8,128)(2,1)}), bf16[4,128,256]{1,2,0:T(8,128)(2,1)}, u32[]{:S(2)}, u32[]{:S(2)}) async-start(bf16[4,128,256]{1,2,0:T(8,128)(2,1)} %stack.10), calls=%async_computation.1 | async-start | bytes 524288 | tf_op jit(solution)/shard_map/all_to_all | solution.py:94
  53.2 6.8 %copy-start.32 = (bf16[1,3,128]{2,1,0:T(4,128)(2,1)S(1)}, bf16[1,3,128]{2,1,0:T(4,128)(2,1)}, u32[]{:S(2)}) copy-start(bf16[1,3,128]{2,1,0:T(4,128)(2,1)} %param.16) | copy-start | bytes 2308
  53.2 8.7 %copy-start.21 = (bf16[1,128,256]{1,2,0:T(8,128)(2,1)S(1)}, bf16[1,128,256]{1,2,0:T(8,128)(2,1)}, u32[]{:S(2)}) copy-start(bf16[1,128,256]{1,2,0:T(8,128)(2,1)} %copy.28) | copy-start | bytes 196612
  53.2 8.6 %copy-start.46 = (f32[128]{0:T(128)S(1)}, f32[128]{0:T(128)}, u32[]{:S(2)}) copy-start(f32[128]{0:T(128)} %get-tuple-element.59) | copy-start | bytes 1540
  57.3 4.6 collective-permute-start.1
  62.6 11.0 %all-to-all-start.2 = ((bf16[4,128,256]{1,2,0:T(8,128)(2,1)}), bf16[4,128,256]{1,2,0:T(8,128)(2,1)}, u32[]{:S(2)}, u32[]{:S(2)}) async-start(bf16[4,128,256]{1,2,0:T(8,128)(2,1)} %stack.11), calls=%async_computation.2 | async-start | bytes 524288 | tf_op jit(solution)/shard_map/all_to_all | solution.py:94
  69.2 77.8 %reduce-scatter.5.cloned.1.call-start = ((), (), s32[]{:S(2)}) async-start(), calls=%async_computation.7 | async-start | bytes 655360 | tf_op jit(solution)/shard_map/reduce_scatter | solution.py:159
  110.3 36.7 %copy-start.44 = (f32[128]{0:T(128)S(1)}, f32[128]{0:T(128)}, u32[]{:S(2)}) copy-start(f32[128]{0:T(128)} %get-tuple-element.58) | copy-start | bytes 1540
  111.4 81.2 %reduce-scatter.7.cloned.1.call-start = ((), (), s32[]{:S(2)}) async-start(), calls=%async_computation.8 | async-start | bytes 655360 | tf_op jit(solution)/shard_map/reduce_scatter | solution.py:159
  148.6 6.1 %collective-permute-start.2 = (bf16[128,256]{0,1:T(8,128)(2,1)S(1)}, bf16[128,256]{0,1:T(8,128)(2,1)S(1)}, u32[]{:S(2)}, u32[]{:S(2)}) collective-permute-start(bf16[128,256]{0,1:T(8,128)(2,1)S(1)} %get-tuple-element.18), channel_id=1, source_target_pairs={{4,0},{5,1},{6,2},{7,3},{12,8},{13,9},{14,10},{15,11},{20,16},{21,... | collective-permute-start | bytes 196616 | tf_op jit(solution)/shard_map/ppermute | solution.py:16
  151.0 6.8 %copy-start.2 = (bf16[4608,512]{0,1:T(8,128)(2,1)}, bf16[4608,512]{0,1:T(8,128)(2,1)S(1)}, u32[]{:S(2)}) copy-start(bf16[4608,512]{0,1:T(8,128)(2,1)S(1)} %select_dynamic-update-slice_fusion.2) | copy-start | bytes 14155780
  159.9 32.7 %copy-start.42 = (f32[128]{0:T(128)S(1)}, f32[128]{0:T(128)}, u32[]{:S(2)}) copy-start(f32[128]{0:T(128)} %get-tuple-element.62) | copy-start | bytes 1540
  159.9 79.4 %reduce-scatter.11.cloned.1.call-start = ((), (), s32[]{:S(2)}) async-start(), calls=%async_computation.10 | async-start | bytes 655360 | tf_op jit(solution)/shard_map/reduce_scatter | solution.py:159
  194.2 6.3 %copy-start.9 = (f32[2,256,128]{2,1,0:T(8,128)S(1)}, f32[2,256,128]{2,1,0:T(8,128)}, u32[]{:S(2)}) copy-start(f32[2,256,128]{2,1,0:T(8,128)} %copy-done.7) | copy-start | bytes 786436
  194.2 6.3 %copy-start.13 = (bf16[128,512]{0,1:T(8,128)(2,1)S(1)}, bf16[128,512]{0,1:T(8,128)(2,1)}, u32[]{:S(2)}) copy-start(bf16[128,512]{0,1:T(8,128)(2,1)} %copy-done.12) | copy-start | bytes 393220
  194.2 6.3 %copy-start.43 = (f32[128]{0:T(128)S(1)}, f32[128]{0:T(128)}, u32[]{:S(2)}) copy-start(f32[128]{0:T(128)} %get-tuple-element.66) | copy-start | bytes 1540
  194.2 6.3 %collective-permute-start.3 = (bf16[128,256]{0,1:T(8,128)(2,1)S(1)}, bf16[128,256]{0,1:T(8,128)(2,1)S(1)}, u32[]{:S(2)}, u32[]{:S(2)}) collective-permute-start(bf16[128,256]{0,1:T(8,128)(2,1)S(1)} %get-tuple-element.16), channel_id=1, source_target_pairs={{4,0},{5,1},{6,2},{7,3},{12,8},{13,9},{14,10},{15,11},{20,16},{21,... | collective-permute-start | bytes 196616 | tf_op jit(solution)/shard_map/ppermute | solution.py:16
  205.0 246.1 %reduce-scatter.9.cloned.1.call-start = ((), (), s32[]{:S(2)}) async-start(), calls=%async_computation.9 | async-start | bytes 1216512 | tf_op jit(solution)/shard_map/reduce_scatter | solution.py:171
  207.1 5.0 %copy-start.18 = (bf16[2,128,256]{1,2,0:T(8,128)(2,1)S(1)}, bf16[2,128,256]{1,2,0:T(8,128)(2,1)}, u32[]{:S(2)}) copy-start(bf16[2,128,256]{1,2,0:T(8,128)(2,1)} %get-tuple-element.15) | copy-start | bytes 393220
  207.1 32.2 %copy-start.41 = (f32[128]{0:T(128)S(1)}, f32[128]{0:T(128)}, u32[]{:S(2)}) copy-start(f32[128]{0:T(128)} %get-tuple-element.57) | copy-start | bytes 1540
  (34 other events, 86.7 us)
Sparse Core Ops, SparseCore 0:
  111.6 35.3 reduce-scatter.4
  160.0 32.5 reduce-scatter.6
  205.1 34.2 reduce-scatter.10
  243.0 207.9 reduce-scatter.8
